TPU v7x, 32 devices: a whole 2x2x4 slice. The times are simulated.
32 devices in a mesh: occ: 8 (over z, x), aux: 4 (over y, core).
Axes of the slice: x: 2, y: 2, z: 4, core: 2. Of those that a mesh axis runs over, the one named last changes fastest.
Arguments:
- int_tiles: bfloat16 [32, 64, 128, 256], P('occ', 'aux'), may hold values from -0.5 to 0.5
- tile_ids: int32 [32, 64], P('occ', 'aux'), may hold values from 0 to 79, as said below
- tile_counts: int32 [32, 4], P('occ', 'aux'), may hold values from 8 to 16, as said below
- pair_list: int32 [64, 2], P('occ'), may hold values from 0 to 3
- occ_energy: float32 [32], replicated, may hold values from -2 to -0.5
- vir_energy: float32 [256], replicated, may hold values from 0.2 to 3
Outputs:
- gamma_tiles: bfloat16 [32, 64, 128, 256], P('occ', 'aux')
- density: float32 [256, 256], P('aux')
Inputs may be any that keep to these rules, and one draw needn't show every extreme that they name: `tile_ids`: within one orbital and one aux index's share the 16 tile numbers are distinct. Only the first tile_counts slots of a share are live; tiles and numbers of the others are never read. `pair_list`: column 0 indexes the asking occ index's orbitals, column 1 those of occ index r.
All inputs are finite; a program needn't handle non-finite values.
Results may differ from a plain program's by a relative error of at most 0.0085.
Values may be sent and summed in bfloat16 or wider, within the bound.
A program may use at most 256 MiB of HBM per device.

v0:
```python
import jax
import jax.numpy as jnp
from jax import lax
from jax.sharding import PartitionSpec as P


def amplitudes(coulomb, energy_pair, vir_energy):
    denominator = energy_pair[:, None, None] - vir_energy[None, :, None] - vir_energy[None, None, :]
    amplitude = coulomb / denominator
    return (amplitude, 2.0 * amplitude - jnp.swapaxes(amplitude, 1, 2))


def density_terms(amplitude_left, amplitude_right, spin_mixed):
    first_term = jnp.einsum(
        "rac,rbc->ab", amplitude_left, spin_mixed, precision=lax.Precision.HIGHEST
    )
    second_term = jnp.einsum(
        "rca,rcb->ab", amplitude_right, spin_mixed, precision=lax.Precision.HIGHEST
    )
    return first_term + second_term


def per_device(int_tiles, tile_ids, tile_counts, pair_list, occ_energy, vir_energy):
    peer_count = lax.axis_size("occ")
    group_count = lax.axis_size("aux")
    orb_count = int_tiles.shape[0]
    slot_count = int_tiles.shape[1]
    tile_rows = int_tiles.shape[2]
    virt_width = int_tiles.shape[3]
    pair_count = pair_list.shape[0]
    per_peer = pair_count // peer_count
    block_shape = (peer_count, per_peer, slot_count, tile_rows, virt_width)
    my_first = lax.axis_index("occ") * orb_count
    counts = tile_counts[:, 0]
    source = jnp.arange(pair_count, dtype=jnp.int32) // per_peer
    wanted = pair_list[:, 1]
    asked_for = lax.all_to_all(
        wanted.reshape(peer_count, per_peer), "occ", split_axis=0, concat_axis=0, tiled=True
    ).reshape(pair_count)
    arrived = (
        lax.all_to_all(
            int_tiles[asked_for].reshape(block_shape),
            "occ",
            split_axis=0,
            concat_axis=0,
            tiled=True,
        ),
        lax.all_to_all(
            tile_ids[asked_for].reshape(peer_count, per_peer, slot_count),
            "occ",
            split_axis=0,
            concat_axis=0,
            tiled=True,
        ),
        lax.all_to_all(
            counts[asked_for].reshape(peer_count, per_peer),
            "occ",
            split_axis=0,
            concat_axis=0,
            tiled=True,
        ),
    )
    here_index = pair_list[:, 0]
    there_global = source * orb_count + wanted
    there_tiles, there_ids, there_counts = arrived
    there_tiles = there_tiles.reshape(pair_count, slot_count, tile_rows, virt_width)
    there_ids = there_ids.reshape(pair_count, slot_count)
    there_counts = there_counts.reshape(pair_count)
    energy_pair = occ_energy[my_first + here_index] + occ_energy[there_global]
    slot_range = jnp.arange(slot_count, dtype=jnp.int32)

    def intersection_of(pair_index):
        here_orb = here_index[pair_index]
        here_live = slot_range < counts[here_orb]
        there_live = slot_range < there_counts[pair_index]
        same_tile = tile_ids[here_orb][:, None] == there_ids[pair_index][None, :]
        intersection = (same_tile & here_live[:, None] & there_live[None, :]).astype(jnp.bfloat16)
        return (int_tiles[here_orb], intersection)

    def rows_of_there(intersection, pair_index):
        return jnp.einsum(
            "st,tpb->spb", intersection, there_tiles[pair_index], preferred_element_type=jnp.float32
        ).astype(jnp.bfloat16)

    def coulomb_term(running, pair_index):
        here_block, intersection = intersection_of(pair_index)
        rows_there = rows_of_there(intersection, pair_index)
        term = lax.dot_general(
            here_block.reshape(-1, virt_width),
            rows_there.reshape(-1, virt_width),
            (((0,), (0,)), ((), ())),
            preferred_element_type=jnp.float32,
        )
        return (running, term)

    pair_range = jnp.arange(pair_count, dtype=jnp.int32)
    unused, partial_terms = lax.scan(coulomb_term, 0, pair_range)
    coulomb = lax.psum(partial_terms, "aux")
    amplitude, spin_mixed = amplitudes(coulomb, energy_pair, vir_energy)
    row_block = virt_width // group_count
    row_start = lax.axis_index("aux") * row_block
    amplitude_rows = lax.dynamic_slice_in_dim(amplitude, row_start, row_block, 1)
    amplitude_cols = lax.dynamic_slice_in_dim(amplitude, row_start, row_block, 2)
    density = density_terms(amplitude_rows, amplitude_cols, spin_mixed)
    weights = spin_mixed.astype(jnp.bfloat16)
    density = lax.psum(density.astype(jnp.bfloat16), "occ").astype(jnp.float32)
    part_shape = (slot_count, tile_rows, virt_width)

    def gamma_term(running, pair_index):
        here_block, intersection = intersection_of(pair_index)
        rows_there = rows_of_there(intersection, pair_index)
        rows_here = jnp.einsum(
            "st,spa->tpa", intersection, here_block, preferred_element_type=jnp.float32
        ).astype(jnp.bfloat16)
        pair_weights = weights[pair_index]
        here_part = lax.dot_general(
            rows_there.reshape(-1, virt_width),
            pair_weights,
            (((1,), (1,)), ((), ())),
            preferred_element_type=jnp.float32,
        )
        there_part = jnp.dot(
            rows_here.reshape(-1, virt_width), pair_weights, preferred_element_type=jnp.float32
        )
        return (
            running,
            (
                here_part.astype(jnp.bfloat16).reshape(part_shape),
                there_part.astype(jnp.bfloat16).reshape(part_shape),
            ),
        )

    unused, parts = lax.scan(gamma_term, 0, pair_range)
    here_parts, there_parts = parts
    returned = lax.all_to_all(
        there_parts.reshape(block_shape), "occ", split_axis=0, concat_axis=0, tiled=True
    ).reshape(pair_count, slot_count, tile_rows, virt_width)
    gamma_sum = jnp.zeros((orb_count, slot_count, tile_rows, virt_width), jnp.float32)
    gamma_sum = gamma_sum.at[here_index].add(here_parts.astype(jnp.float32))
    gamma_sum = gamma_sum.at[asked_for].add(returned.astype(jnp.float32))
    return (gamma_sum.astype(jnp.bfloat16), density)


def solution(mesh):
    placed = (
        P("occ", "aux", None, None),
        P("occ", "aux"),
        P("occ", "aux"),
        P("occ", None),
        P(),
        P(),
    )
    return jax.shard_map(
        per_device,
        mesh=mesh,
        in_specs=placed,
        out_specs=(P("occ", "aux", None, None), P("aux", None)),
        check_vma=False,
    )
```

profile of v0, /device:TPU:0, one launch (start us, length us, event | category | flops | bytes accessed | tf_op | source)
XLA Modules:
  0.0 811.5 jit_solution(979739568386542824)
XLA Ops:
  8.0 13.5 %all_to_all.36 = s32[8,1,1]{2,1,0:T(1,128)S(1)} all-to-all(s32[8,1,1]{2,1,0:T(1,128)S(1)} %copy.47), channel_id=1, replica_groups=mesh['occ'=8,'aux'=4] {'occ'}, dimensions={0} | all-to-all | bytes 64 | tf_op jit(solution)/shard_map/all_to_all | solution.py:37
  23.8 3.3 all-to-all-start.2
  27.1 6.9 gather_fusion.2
  34.0 6.0 all-to-all-start.3
  41.1 180.3 %all-to-all-done.3 = bf16[8,1,16,128,256]{4,3,2,1,0:T(8,128)(2,1)} async-done(((bf16[8,1,16,128,256]{4,3,2,1,0:T(8,128)(2,1)}), bf16[8,1,16,128,256]{4,3,2,1,0:T(8,128)(2,1)}, u32[]{:S(2)}, u32[]{:S(2)}) %all-to-all-start.3) | async-done | bytes 8388640 | tf_op jit(solution)/shard_map/all_to_all | solution.py:41
  221.4 3.6 all-to-all-start.1
  225.4 11.8 %copy.53 = bf16[8,16,128,256]{3,1,2,0:T(8,128)(2,1)} copy(bf16[8,16,128,256]{3,2,1,0:T(8,128)(2,1)} %bitcast.11) | data formatting | bytes 16777216
  237.2 96.8 %while.26 = (s32[]{:T(128)}, f32[8,256,256]{2,1,0:T(8,128)}, s32[8]{0:T(128)S(1)}, s32[8]{0:T(128)S(1)}, bf16[4,16,128,256]{3,2,1,0:T(8,128)(2,1)}, /*index=5*/s...) while((s32[]{:T(128)}, f32[8,256,256]{2,1,0:T(8,128)}, ...), condition=%wide.region_1.2_spmd.clone.clone, body=%wide.region_0.1_spmd.clone.clone.sunk | while | flops 285737760 | bytes 8651985 | solution.py:97
  335.5 51.5 %all-reduce.2.cloned.1.call-done = f32[8,256,256]{2,1,0:T(8,128)} async-done(((f32[8,256,256]{2,1,0:T(8,128)}), f32[8,256,256]{2,1,0:T(8,128)}) %all-reduce.2.cloned.1.call-update) | async-done | bytes 2097168 | tf_op jit(solution)/shard_map/psum | solution.py:98
  387.0 1.9 subtract_divide_fusion
  388.9 1.8 copy.52
  390.7 2.7 fusion.49
  393.4 115.8 %while.27 = (s32[]{:T(128)}, bf16[8,16,128,256]{3,2,1,0:T(8,128)(2,1)}, bf16[8,16,128,256]{3,2,1,0:T(8,128)(2,1)}, s32[8]{0:T(128)S(1)}, s32[8]{0:T(128)S(1)}, /...) while((s32[]{:T(128)}, ...), condition=%wide.region_4.5_spmd.clone.clone, body=%wide.region_3.4_spmd.clone.clone.sunk | while | flops 572524032 | bytes 19137928 | solution.py:133
  461.8 1.8 convolution_convert_fusion.13
  476.3 1.8 convolution_convert_fusion.13
  509.2 5.5 all-to-all-start.4
  514.8 11.6 %convert_element_type.39 = f32[8,16,128,256]{3,2,1,0:T(8,128)} convert(bf16[8,16,128,256]{3,2,1,0:T(8,128)(2,1)} %get-tuple-element.134) | non-fusion elementwise | flops 4194304 | bytes 25165824 | tf_op jit(solution)/shard_map/convert_element_type | solution.py:139
  527.7 2.5 fusion.40
  530.2 190.8 %psum.15 = bf16[64,256]{1,0:T(8,128)(2,1)S(1)} all-reduce(bf16[64,256]{1,0:T(8,128)(2,1)S(1)} %fusion.40), channel_id=1, replica_groups=mesh['occ'=8,'aux'=4] {'occ'}, use_global_device_ids=true, to_apply=%region_7.8 | all-reduce | flops 16384 | bytes 65536 | tf_op jit(solution)/shard_map/psum | solution.py:106
  721.6 4.3 broadcast_in_dim.16
  725.9 30.6 %scatter_fusion = f32[4,16,128,256]{3,2,1,0:T(8,128)} fusion(f32[4,16,128,256]{3,2,1,0:T(8,128)} %broadcast_in_dim.16, s32[8]{0:T(128)S(1)} %get-tuple-element.370, f32[8,16,128,256]{3,2,1,0:T(8,128)} %convert_element_type.39), kind=kCustom, calls=%fused_computation.5 | custom fusion | flops 4194304 | bytes 50331680 | tf_op jit(solution)/shard_map/scatter-add | solution.py:139
  756.5 11.5 %bitcast_convert_fusion = f32[8,16,128,256]{3,2,1,0:T(8,128)} fusion(bf16[8,1,16,128,256]{4,3,2,1,0:T(8,128)(2,1)} %all-to-all-done.4), kind=kLoop, calls=%fused_computation.64 | loop fusion | flops 4194304 | bytes 25165824 | tf_op jit(solution)/shard_map/convert_element_type | solution.py:140
  768.0 30.6 %scatter_fusion.1 = f32[4,16,128,256]{3,2,1,0:T(8,128)} fusion(f32[4,16,128,256]{3,2,1,0:T(8,128)} %scatter_fusion, s32[8]{0:T(128)S(1)} %fusion.44, f32[8,16,128,256]{3,2,1,0:T(8,128)} %bitcast_convert_fusion), kind=kCustom, calls=%fused_computation.6 | custom fusion | flops 4194304 | bytes 50331680 | tf_op jit(solution)/shard_map/scatter-add | solution.py:140
  798.6 6.0 convert_element_type.42
  (244 shorter events, 154.6 us)
Async XLA Ops:
  7.2 326.9 %copy-start = (f32[32]{0:T(128)S(1)}, f32[32]{0:T(128)}, u32[]{:S(2)}) copy-start(f32[32]{0:T(128)} %param.14) | copy-start | bytes 388
  23.8 10.2 %all-to-all-start.2 = ((s32[8,1,1]{2,1,0:T(1,128)}), s32[8,1,1]{2,1,0:T(1,128)S(1)}, u32[]{:S(2)}, u32[]{:S(2)}) async-start(s32[8,1,1]{2,1,0:T(1,128)} %copy.49), calls=%async_computation.2 | async-start | bytes 8192 | tf_op jit(solution)/shard_map/all_to_all | solution.py:55
  34.0 6.0 copy-start.4
  34.0 187.5 %all-to-all-start.3 = ((bf16[8,1,16,128,256]{4,3,2,1,0:T(8,128)(2,1)}), bf16[8,1,16,128,256]{4,3,2,1,0:T(8,128)(2,1)}, u32[]{:S(2)}, u32[]{:S(2)}) async-start(bf16[8,1,16,128,256]{4,3,2,1,0:T(8,128)(2,1)} %bitcast.165), calls=%async_computation.3 | async-start | bytes 16777216 | tf_op jit(solution)/shard_map/all_to_all | solution.py:41
  221.4 15.7 %all-to-all-start.1 = ((s32[8,1,16]{2,1,0:T(1,128)}), s32[8,1,16]{2,1,0:T(1,128)S(1)}, u32[]{:S(2)}, u32[]{:S(2)}) async-start(s32[8,1,16]{2,1,0:T(1,128)} %bitcast.5), calls=%async_computation.1 | async-start | bytes 8192 | tf_op jit(solution)/shard_map/all_to_all | solution.py:48
  225.1 161.9 %all-reduce.2.cloned.1.call-start = ((), (), s32[]{:S(2)}) async-start(), calls=%async_computation.5 | async-start | bytes 4194304 | tf_op jit(solution)/shard_map/psum | solution.py:98
  225.3 11.8 %copy-start.2 = (s32[4,1]{0,1:T(1,128)S(1)}, s32[4,1]{0,1:T(1,128)}, u32[]{:S(2)}) copy-start(s32[4,1]{0,1:T(1,128)} %param.12) | copy-start | bytes 52
  237.2 98.2 %copy-start.5 = (f32[256]{0:T(256)S(1)}, f32[256]{0:T(256)}, u32[]{:S(2)}) copy-start(f32[256]{0:T(256)} %param.15) | copy-start | bytes 3076
  509.2 247.3 %all-to-all-start.4 = ((bf16[8,1,16,128,256]{4,3,2,1,0:T(8,128)(2,1)}), bf16[8,1,16,128,256]{4,3,2,1,0:T(8,128)(2,1)}, u32[]{:S(2)}, u32[]{:S(2)}) async-start(bf16[8,1,16,128,256]{4,3,2,1,0:T(8,128)(2,1)} %bitcast.166), calls=%async_computation.4 | async-start | bytes 16777216 | tf_op jit(solution)/shard_map/all_to_all | solution.py:135
  514.8 11.6 %copy-start.3 = (f32[8,256,256]{1,2,0:T(8,128)S(1)}, f32[8,256,256]{1,2,0:T(8,128)}, u32[]{:S(2)}) copy-start(f32[8,256,256]{1,2,0:T(8,128)} %copy.52) | copy-start | bytes 6291460
  768.0 36.6 %copy-start.1 = (f32[32]{0:T(128)S(1)}, f32[32]{0:T(128)}, u32[]{:S(2)}) copy-start(f32[32]{0:T(128)} %param.14) | copy-start | bytes 388
Sparse Core Ops, SparseCore 0:
  334.2 52.7 all-reduce.1
where the time goes:
time: 815 us; the launch traced here: 811 us
  waiting for transfers between devices  232 us (28%)
  blocking collectives  204 us (25%)
  other arithmetic  117 us (14%)
  local copies, waits for them, and re-layouts  109 us (13%)
  loops' own time  62.4 us (8%)
  matrix products  54.3 us (7%)
  starting transfers between devices  18.5 us (2%)
  between operations  14.2 us (2%)
    psum x1, blocking collectives, per_device(): density = lax.psum(density.astype(jnp.bfloat16), 'occ').astype(jnp.float32)  191 us
    all_to_all x1, waiting for transfers between devices, per_device(): lax.all_to_all(int_tiles[asked_for].reshape(block_shape), 'occ', split_ax...  180 us
    psum x1, waiting for transfers between devices, per_device(): coulomb = lax.psum(partial_terms, 'aux')  51.5 us
    another operation x1, loops' own time, per_device(): unused, partial_terms = lax.scan(coulomb_term, 0, pair_range)  31.4 us
    another operation x1, loops' own time, per_device(): unused, parts = lax.scan(gamma_term, 0, pair_range)  31 us
    scatter-add x1, other arithmetic, per_device(): gamma_sum = gamma_sum.at[here_index].add(here_parts.astype(jnp.float32))  30.6 us
    scatter-add x1, other arithmetic, per_device(): gamma_sum = gamma_sum.at[asked_for].add(returned.astype(jnp.float32))  30.6 us
    dot_general x16, matrix products, rows_of_there(): jnp.einsum('st,tpb->spb', intersection, there_tiles[pair_index], preferre...  27.9 us
  transfers between devices with their start and end apart: 5, of which 2 were waited for; matrix products, arithmetic and copies ran while one was open for 9% of the time, Pallas kernels for 0%

commit v1 on v0

--- a/solution.py
+++ b/solution.py
@@ -95,7 +95,7 @@
 
     pair_range = jnp.arange(pair_count, dtype=jnp.int32)
     unused, partial_terms = lax.scan(coulomb_term, 0, pair_range)
-    coulomb = lax.psum(partial_terms, "aux")
+    coulomb = jnp.sum(lax.all_gather(partial_terms, "aux"), axis=0)
     amplitude, spin_mixed = amplitudes(coulomb, energy_pair, vir_energy)
     row_block = virt_width // group_count
     row_start = lax.axis_index("aux") * row_block

time: 815 us -> 843 us (1.034)
  blocking collectives: 204 us -> 214 us
    all_gather x0 -> x1, waiting for transfers between devices: none -> 58.4 us  [per_device(): coulomb = jnp.sum(lax.all_gather(partial_terms, 'aux'), axis=0)]
    psum x1 -> x0, waiting for transfers between devices: 51.5 us -> none  [per_device(): coulomb = lax.psum(partial_terms, 'aux')]
    psum x1, blocking collectives: 191 us -> 200 us  [per_device(): density = lax.psum(density.astype(jnp.bfloat16), 'occ').astype(jnp.float32)]
where the time goes in v1:
time: 843 us; the launch traced here: 840 us
  waiting for transfers between devices  239 us (28%)
  blocking collectives  214 us (25%)
  other arithmetic  122 us (14%)
  local copies, waits for them, and re-layouts  112 us (13%)
  loops' own time  64.3 us (8%)
  matrix products  57 us (7%)
  starting transfers between devices  18.5 us (2%)
  between operations  14.2 us (2%)
    psum x1, blocking collectives, per_device(): density = lax.psum(density.astype(jnp.bfloat16), 'occ').astype(jnp.float32)  200 us
    all_to_all x1, waiting for transfers between devices, per_device(): lax.all_to_all(int_tiles[asked_for].reshape(block_shape), 'occ', split_ax...  180 us
    all_gather x1, waiting for transfers between devices, per_device(): coulomb = jnp.sum(lax.all_gather(partial_terms, 'aux'), axis=0)  58.4 us
    another operation x1, loops' own time, per_device(): unused, parts = lax.scan(gamma_term, 0, pair_range)  32.9 us
    another operation x1, loops' own time, per_device(): unused, partial_terms = lax.scan(coulomb_term, 0, pair_range)  31.4 us
    scatter-add x1, other arithmetic, per_device(): gamma_sum = gamma_sum.at[here_index].add(here_parts.astype(jnp.float32))  30.6 us
    scatter-add x1, other arithmetic, per_device(): gamma_sum = gamma_sum.at[asked_for].add(returned.astype(jnp.float32))  30.6 us
    dot_general x16, matrix products, rows_of_there(): jnp.einsum('st,tpb->spb', intersection, there_tiles[pair_index], preferre...  27.9 us
  transfers between devices with their start and end apart: 5, of which 2 were waited for; matrix products, arithmetic and copies ran while one was open for 9% of the time, Pallas kernels for 0%

profile of v1, /device:TPU:0, one launch (start us, length us, event | category | flops | bytes accessed | tf_op | source)
XLA Modules:
  0.0 840.0 jit_solution(8356907049899974143)
XLA Ops:
  8.0 13.5 %all_to_all.36 = s32[8,1,1]{2,1,0:T(1,128)S(1)} all-to-all(s32[8,1,1]{2,1,0:T(1,128)S(1)} %copy.38), channel_id=1, replica_groups=mesh['occ'=8,'aux'=4] {'occ'}, dimensions={0} | all-to-all | bytes 64 | tf_op jit(solution)/shard_map/all_to_all | solution.py:37
  23.8 3.3 all-to-all-start.2
  27.1 6.9 gather_fusion.2
  34.0 6.0 all-to-all-start.3
  41.1 180.3 %all-to-all-done.3 = bf16[8,1,16,128,256]{4,3,2,1,0:T(8,128)(2,1)} async-done(((bf16[8,1,16,128,256]{4,3,2,1,0:T(8,128)(2,1)}), bf16[8,1,16,128,256]{4,3,2,1,0:T(8,128)(2,1)}, u32[]{:S(2)}, u32[]{:S(2)}) %all-to-all-start.3) | async-done | bytes 8388640 | tf_op jit(solution)/shard_map/all_to_all | solution.py:41
  221.4 3.6 all-to-all-start.1
  225.4 11.8 %copy.44 = bf16[8,16,128,256]{3,1,2,0:T(8,128)(2,1)} copy(bf16[8,16,128,256]{3,2,1,0:T(8,128)(2,1)} %bitcast.11) | data formatting | bytes 16777216
  237.2 97.5 %while.26 = (s32[]{:T(128)}, f32[8,256,256]{2,1,0:T(8,128)}, s32[8]{0:T(128)S(1)}, s32[8]{0:T(128)S(1)}, bf16[4,16,128,256]{3,2,1,0:T(8,128)(2,1)}, /*index=5*/s...) while((s32[]{:T(128)}, f32[8,256,256]{2,1,0:T(8,128)}, ...), condition=%wide.region_1.2_spmd.clone.clone, body=%wide.region_0.1_spmd.clone.clone.sunk | while | flops 285737760 | bytes 8651985 | solution.py:97
  336.1 58.4 %all-gather.3.cloned.1.call-done = f32[32,256,256]{2,1,0:T(8,128)} async-done(((f32[8,256,256]{2,1,0:T(8,128)}), f32[32,256,256]{2,1,0:T(8,128)}) %all-gather.3.cloned.1.call-update) | async-done | bytes 8388624 | tf_op jit(solution)/shard_map/all_gather | solution.py:98
  394.5 4.3 reduce_sum.11
  400.2 1.8 copy.43
  402.0 4.2 fusion.50
  406.2 119.6 %while.27 = (s32[]{:T(128)}, bf16[8,16,128,256]{3,2,1,0:T(8,128)(2,1)}, bf16[8,16,128,256]{3,2,1,0:T(8,128)(2,1)}, s32[8]{0:T(128)S(1)}, s32[8]{0:T(128)S(1)}, /...) while((s32[]{:T(128)}, ...), condition=%wide.region_4.5_spmd.clone.clone, body=%wide.region_3.4_spmd.clone.clone.sunk | while | flops 572524032 | bytes 19137928 | solution.py:133
  476.9 1.8 convolution_convert_fusion.13
  525.8 5.5 all-to-all-start.4
  531.3 3.1 convolution_bitcast_fusion.2
  534.4 3.5 fusion.41
  537.9 200.2 %psum.7 = bf16[64,256]{1,0:T(8,128)(2,1)S(1)} all-reduce(bf16[64,256]{1,0:T(8,128)(2,1)S(1)} %fusion.41), channel_id=1, replica_groups=mesh['occ'=8,'aux'=4] {'occ'}, use_global_device_ids=true, to_apply=%region_7.8 | all-reduce | flops 16384 | bytes 65536 | tf_op jit(solution)/shard_map/psum | solution.py:106
  738.8 11.5 %convert_element_type.39 = f32[8,16,128,256]{3,2,1,0:T(8,128)} convert(bf16[8,16,128,256]{3,2,1,0:T(8,128)(2,1)} %get-tuple-element.134) | non-fusion elementwise | flops 4194304 | bytes 25165824 | tf_op jit(solution)/shard_map/convert_element_type | solution.py:139
  750.2 4.3 broadcast_in_dim.16
  754.5 30.6 %scatter_fusion = f32[4,16,128,256]{3,2,1,0:T(8,128)} fusion(f32[4,16,128,256]{3,2,1,0:T(8,128)} %broadcast_in_dim.16, s32[8]{0:T(128)S(1)} %get-tuple-element.373, f32[8,16,128,256]{3,2,1,0:T(8,128)} %convert_element_type.39), kind=kCustom, calls=%fused_computation.5 | custom fusion | flops 4194304 | bytes 50331680 | tf_op jit(solution)/shard_map/scatter-add | solution.py:139
  785.1 11.5 %bitcast_convert_fusion = f32[8,16,128,256]{3,2,1,0:T(8,128)} fusion(bf16[8,1,16,128,256]{4,3,2,1,0:T(8,128)(2,1)} %all-to-all-done.4), kind=kLoop, calls=%fused_computation.64 | loop fusion | flops 4194304 | bytes 25165824 | tf_op jit(solution)/shard_map/convert_element_type | solution.py:140
  796.5 30.6 %scatter_fusion.1 = f32[4,16,128,256]{3,2,1,0:T(8,128)} fusion(f32[4,16,128,256]{3,2,1,0:T(8,128)} %scatter_fusion, s32[8]{0:T(128)S(1)} %fusion.45, f32[8,16,128,256]{3,2,1,0:T(8,128)} %bitcast_convert_fusion), kind=kCustom, calls=%fused_computation.6 | custom fusion | flops 4194304 | bytes 50331680 | tf_op jit(solution)/shard_map/scatter-add | solution.py:140
  827.1 6.0 convert_element_type.42
  (244 shorter events, 158.9 us)
Async XLA Ops:
  7.2 327.6 %copy-start = (f32[32]{0:T(128)S(1)}, f32[32]{0:T(128)}, u32[]{:S(2)}) copy-start(f32[32]{0:T(128)} %param.14) | copy-start | bytes 388
  23.8 10.2 %all-to-all-start.2 = ((s32[8,1,1]{2,1,0:T(1,128)}), s32[8,1,1]{2,1,0:T(1,128)S(1)}, u32[]{:S(2)}, u32[]{:S(2)}) async-start(s32[8,1,1]{2,1,0:T(1,128)} %copy.40), calls=%async_computation.2 | async-start | bytes 8192 | tf_op jit(solution)/shard_map/all_to_all | solution.py:55
  34.0 6.0 copy-start.4
  34.0 187.5 %all-to-all-start.3 = ((bf16[8,1,16,128,256]{4,3,2,1,0:T(8,128)(2,1)}), bf16[8,1,16,128,256]{4,3,2,1,0:T(8,128)(2,1)}, u32[]{:S(2)}, u32[]{:S(2)}) async-start(bf16[8,1,16,128,256]{4,3,2,1,0:T(8,128)(2,1)} %bitcast.165), calls=%async_computation.3 | async-start | bytes 16777216 | tf_op jit(solution)/shard_map/all_to_all | solution.py:41
  221.4 15.8 %all-to-all-start.1 = ((s32[8,1,16]{2,1,0:T(1,128)}), s32[8,1,16]{2,1,0:T(1,128)S(1)}, u32[]{:S(2)}, u32[]{:S(2)}) async-start(s32[8,1,16]{2,1,0:T(1,128)} %bitcast.5), calls=%async_computation.1 | async-start | bytes 8192 | tf_op jit(solution)/shard_map/all_to_all | solution.py:48
  225.1 169.4 %all-gather.3.cloned.1.call-start = ((), (), s32[]{:S(2)}) async-start(), calls=%async_computation.5 | async-start | bytes 10485760 | tf_op jit(solution)/shard_map/all_gather | solution.py:98
  225.4 11.8 %copy-start.2 = (s32[4,1]{0,1:T(1,128)S(1)}, s32[4,1]{0,1:T(1,128)}, u32[]{:S(2)}) copy-start(s32[4,1]{0,1:T(1,128)} %param.12) | copy-start | bytes 52
  237.2 98.8 %copy-start.5 = (f32[256]{0:T(256)S(1)}, f32[256]{0:T(256)}, u32[]{:S(2)}) copy-start(f32[256]{0:T(256)} %param.15) | copy-start | bytes 3076
  398.8 1.4 copy-start.3
  525.8 259.3 %all-to-all-start.4 = ((bf16[8,1,16,128,256]{4,3,2,1,0:T(8,128)(2,1)}), bf16[8,1,16,128,256]{4,3,2,1,0:T(8,128)(2,1)}, u32[]{:S(2)}, u32[]{:S(2)}) async-start(bf16[8,1,16,128,256]{4,3,2,1,0:T(8,128)(2,1)} %bitcast.166), calls=%async_computation.4 | async-start | bytes 16777216 | tf_op jit(solution)/shard_map/all_to_all | solution.py:135
  796.5 36.6 %copy-start.1 = (f32[32]{0:T(128)S(1)}, f32[32]{0:T(128)}, u32[]{:S(2)}) copy-start(f32[32]{0:T(128)} %param.14) | copy-start | bytes 388
Sparse Core Ops, SparseCore 0:
  334.8 59.6 all-gather.2
